TPU v7x, 512 devices: a whole 4x8x8 slice. The times are simulated.
512 devices in a mesh: mem: 4 (over x), lat: 4 (over y_hi, core), lon: 32 (over z, y_lo).
Axes of the slice: x: 4, y: 8 (y_hi: 2, y_lo: 4; y = y_hi * 4 + y_lo), z: 8, core: 2. Of those that a mesh axis runs over, the one named last changes fastest.
Arguments:
- initial_temp: float32 [100, 128, 512], P(None, 'lon', 'lat'), may hold values from -6 to 6
- land_mask: int32 [128, 512], P('lon', 'lat'), may hold values 0 or 1
- pert_table: float32 [16, 100], replicated, may hold values from 0.03 to 0.24
- pert_index: int32 [8], P('mem'), may hold values from 0 to 15
- base_kh: float32 [100], replicated, may hold values from 0.03 to 0.24
- member_mix: bfloat16 [8, 100, 100], P('mem'), may hold values from -0.15625 to 0.15625
- base_mix: bfloat16 [100, 100], replicated, may hold values from -0.15625 to 0.15625
- owner: int32 [32768, 1], P(('lat', 'lon')), may hold values from 0 to 127; in each aligned block of 256 rows (0 to 255, 256 to 511, ...) at most 4 rows name the same one
- column: int32 [32768], P(('lat', 'lon')), may hold values from 0 to 511
- interp_w: float32 [32768, 100], P(('lat', 'lon')), may hold values from 0 to 1
- obs_inv_var: float32 [32768, 100], P(('lat', 'lon')), may hold values from 1 to 16
- observed: float32 [32768, 100], P(('lat', 'lon')), may hold values from -6 to 6
Outputs:
- member_temp: bfloat16 [8, 100, 128, 512], P('mem', None, 'lon', 'lat')
- base_temp: bfloat16 [100, 128, 512], P(None, 'lon', 'lat')
- gram_block: float32 [8, 8], replicated
- projection: float32 [8], replicated
- misfit: float32 [32768, 100], P(('lat', 'lon'))
Inputs may be any that keep to these rules, and one draw needn't show every extreme that they name: Within the records of one device no owner is named more than 4 times, and in every draw some owner is named exactly 4 times by some device's records. The column within the owner's block is the longitude offset times 128 plus the latitude offset.
All inputs are finite; a program needn't handle non-finite values. No bound on the sum of `land_mask` on one device may be relied on, other than what follows from the above.
Results may differ from a plain program's by a relative error of at most 0.012.
Values may be sent and summed in bfloat16 or wider, within the bound.
No kernel may reach another device: no remote copies, remote signals or barrier semaphores. Data moves between devices by JAX's collectives and lax.ppermute only.
A program may use at most 64 MiB of HBM per device.

v0:
```python
import functools

import jax
import jax.numpy as jnp
from jax import lax
from jax.experimental import pallas as pl
from jax.experimental.pallas import tpu as pltpu
from jax.sharding import PartitionSpec as P


STEPS = 5
BLOCKS = (4, 5, 4, 6, 4)
K = 100
KP = 128
SPARE = KP - K
CX = 4
CY = 128
CAP = 4
OWN = 128
REC = 256
HALO = 8
ROWS = CY + 2 * HALO
COLS = CX * CY
MEMBERS = 8
RUNS = MEMBERS + 1
MIX = 104
PAIRS = [(a, b) for a in range(MEMBERS) for b in range(a, MEMBERS)]
F32 = jnp.float32
BF16 = jnp.bfloat16
NT = (((1,), (1,)), ((), ()))
NN = (((1,), (0,)), ((), ()))
TN = (((0,), (0,)), ((), ()))
SMEM = pltpu.SMEM
VMEM = pltpu.VMEM


def dot(a, b, dims):
    return lax.dot_general(a, b, dims, preferred_element_type=F32)


def ones_where(cond):
    return jnp.where(cond, 1.0, 0.0).astype(BF16)


def iota(shape, dim):
    return lax.broadcasted_iota(jnp.int32, shape, dim)


def slots_kernel(owner_ref, column_ref, w_ref, iv_ref, ob_ref, out_ref, code_ref, pad, rows3):
    owner = owner_ref[...]
    column = column_ref[...]
    hit = iota((OWN, REC), 0) == owner
    before = ones_where(iota((REC, REC), 0) < iota((REC, REC), 1))
    earlier = dot(ones_where(hit), before, NN)
    rank = jnp.sum(jnp.where(hit, earlier, 0.0), 0, keepdims=True).astype(jnp.int32)
    slot = owner * CAP + rank
    code_ref[...] = slot
    pad[...] = jnp.zeros((3 * KP, REC), F32)
    for group, ref in enumerate((w_ref, iv_ref, ob_ref)):
        pad[group * KP : group * KP + K, :] = ref[...]
    pad[K : K + 1, :] = (column // CY + 1).astype(F32)
    pad[K + 1 : K + 2, :] = (column % CY).astype(F32)
    place = ones_where(iota((OWN * CAP, REC), 0) == slot)
    placed = dot(place, pad[...].astype(BF16), NT)
    for group in range(3):
        rows3[pl.ds(group, OWN * CAP, stride=3), :] = placed[:, group * KP : (group + 1) * KP]
    out_ref[...] = rows3[...].astype(BF16)


def mixes_kernel(index_ref, table_ref, mix_ref, out_ref, pad):
    for j in range(2):
        pad[...] = jnp.zeros((MIX, KP), F32)
        pad[0:K, 0:K] = mix_ref[j].astype(F32)
        kh = table_ref[pl.ds(index_ref[j], 1), :]
        high = kh.astype(BF16).astype(F32)
        pad[K : K + 1, 0:K] = high
        pad[K + 1 : K + 2, 0:K] = kh - high
        packed = pad[...].astype(BF16)
        for copy in range(4):
            out_ref[copy, j] = packed


def window_kernel(
    m_ref, lon_ref, own_ref, near0_ref, near1_ref, far0_ref, far1_ref, recv_ref,
    mixes_ref,
    base_kh_ref, base_mix_ref,
    fields_ref, out_ref,
    start, spread, ping, pong, ocean, kh_pad, mix_pad, one_pad, base_pad, slots, greens, weighted, sums,
    *, scale,
):
    body = pl.ds(8, ROWS)

    def fill(column, cells):
        cells = cells.astype(F32)
        start[column, body, :] = cells
        ocean[column] = jnp.broadcast_to(cells[:, K : K + 1], (ROWS, KP))

    near_side = 1 - lax.rem(lon_ref[0], 2)
    far_side = 1 - lax.rem(lon_ref[0] // 2, 2)
    start[13 * far_side, pl.ds(16, CY), :] = far0_ref[0].astype(F32)
    start[13 * (1 - far_side), pl.ds(16, CY), :] = far1_ref[0].astype(F32)
    for c in range(CX):
        fill(5 + c, own_ref[c])
        fill(1 + 8 * near_side + c, near0_ref[c])
        fill(1 + 8 * (1 - near_side) + c, near1_ref[c])
    kh_pad[...] = jnp.zeros((16, KP), F32)
    mix_pad[...] = jnp.zeros((MEMBERS // 2, 2 * KP, 2 * KP), BF16)
    for member in range(MEMBERS):
        pair, half = member // 2, member % 2
        spot = half * KP
        mix_pad[pair, spot : spot + K, spot : spot + KP] = mixes_ref[pair, half, 0:K, :]
        parts = mixes_ref[pair, half, MIX - 8 : MIX, :].astype(F32)
        kh_pad[member : member + 1, :] = parts[4:5] + parts[5:6]
    kh_pad[MEMBERS : MEMBERS + 1, 0:K] = base_kh_ref[...]
    same = iota((KP, KP), 0) == iota((KP, KP), 1)
    one_pad[...] = jnp.zeros((2 * KP, 2 * KP), BF16)
    one_pad[0:KP, 0:KP] = ones_where(same)
    one_pad[KP:, KP:] = ones_where(same)
    base_pad[...] = jnp.zeros((KP, 2 * KP), BF16)
    base_pad[0:K, 0:K] = base_mix_ref[...]
    base_pad[:, KP:] = ones_where(same)

    for c in range(1, 13):
        spread[c] = (start[c + 1, pl.ds(12, CY + 8), :] + start[c - 1, pl.ds(12, CY + 8), :]) + (
            start[c, pl.ds(13, CY + 8), :] + start[c, pl.ds(11, CY + 8), :]
        )

    for step in range(STEPS):
        source, target = ((ping, pong), (pong, ping))[step % 2]
        row0, count = (12, CY + 8) if step < STEPS - 1 else (16, CY)
        columns, block = 12 - 2 * step, BLOCKS[step]

        def at(run, lon, row, step=step, source=source, count=count):
            if step == 0:
                return start[lon, pl.ds(row, count), :]
            return source[run, lon, pl.ds(row, count), :]

        def rights(run, first, step=step, row0=row0, block=block, at=at):
            kh = kh_pad[pl.ds(run, 1), :]
            keep = 1.0 - 4.0 * kh
            parts = []
            for c in range(block):
                lon = first + c
                if step == 0:
                    around = spread[lon]
                else:
                    around = (at(run, lon + 1, row0) + at(run, lon - 1, row0)) + (
                        at(run, lon, row0 + 1) + at(run, lon, row0 - 1)
                    )
                parts.append(at(run, lon, row0) * keep + around * kh)
            return jnp.concatenate(parts, 0).astype(BF16)

        def put(run, first, mixed, row0=row0, count=count, block=block, at=at, target=target):
            for c in range(block):
                lon = first + c
                open_ = ocean[lon, pl.ds(row0 - 8, count), :] > 0.0
                new = jnp.where(open_, mixed[c * count : (c + 1) * count], at(run, lon, row0))
                target[run, lon, pl.ds(row0, count), :] = new.astype(BF16).astype(F32)

        def advance(pair, first, rights=rights, put=put):
            right = jnp.concatenate([rights(2 * pair, first), rights(2 * pair + 1, first)], 1)
            both = dot(right, mix_pad[pair], NT) + dot(right, one_pad[...], NT)
            put(2 * pair, first, both[:, :KP])
            put(2 * pair + 1, first, both[:, KP:])

        def advance_base(first, rights=rights, put=put):
            right = rights(MEMBERS, first)
            put(MEMBERS, first, dot(jnp.concatenate([right, right], 1), base_pad[...], NT))

        def turn(t, _, step=step, columns=columns, block=block, advance=advance, advance_base=advance_base):
            first = step + 1 + t * block
            for pair in range(MEMBERS // 2):
                advance(pair, first)
            advance_base(first)
            return 0

        if columns == block:
            turn(0, 0)
        else:
            lax.fori_loop(0, columns // block, turn, 0)

    final = pong

    def flat(run):
        return jnp.concatenate([final[run, 5 + c, pl.ds(16, CY), :].astype(BF16) for c in range(CX)], 0)

    for place, run in enumerate((2 * m_ref[0], 2 * m_ref[0] + 1, MEMBERS)):
        for c in range(CX):
            fields_ref[place, c] = final[run, 5 + c, pl.ds(16, CY), :].T[0:K, :].astype(BF16)

    count = OWN * CAP
    slots[...] = recv_ref[...].astype(F32)
    weight = slots[pl.ds(0, count, stride=3), :]
    inv_var = slots[pl.ds(1, count, stride=3), :]
    measured = slots[pl.ds(2, count, stride=3), :]
    at = ((weight[:, K : K + 1] - 1.0) * CY + weight[:, K + 1 : K + 2]).astype(jnp.int32)
    pick = ones_where(at == iota((count, COLS), 1))
    weight = jnp.where(iota((count, KP), 1) < K - 1, weight, 1.0)

    def model(x):
        below = pltpu.roll(x, KP - 1, 1)
        return below + weight * (x - below)

    base = dot(pick, flat(MEMBERS), NN)
    misfit = measured - model(base)
    for pair in range(MEMBERS // 2):
        both = dot(pick, jnp.concatenate([flat(2 * pair), flat(2 * pair + 1)], 1), NN)
        for half in range(2):
            green = model(both[:, half * KP : (half + 1) * KP] - base).astype(BF16).astype(F32)
            greens[2 * pair + half] = green
            weighted[2 * pair + half] = green * inv_var
    sums[...] = jnp.zeros((KP, KP), F32)
    for i, (a, b) in enumerate(PAIRS):
        sums[i : i + 1, :] = jnp.sum(weighted[a] * greens[b], 0, keepdims=True)
    for a in range(MEMBERS):
        sums[len(PAIRS) + a : len(PAIRS) + a + 1, :] = jnp.sum(weighted[a] * misfit, 0, keepdims=True)
    total = jnp.sum(sums[...].T, 0, keepdims=True) * scale
    high = jnp.broadcast_to(total.astype(BF16).astype(F32), (8, KP))
    rest = jnp.broadcast_to(total, (8, KP)) - high
    turn = iota((8, KP), 0) % CAP
    tail = jnp.where(
        turn == 0,
        pltpu.roll(high, K, 1),
        jnp.where(
            turn == 1,
            pltpu.roll(high, K - SPARE, 1),
            jnp.where(turn == 2, pltpu.roll(rest, K, 1), pltpu.roll(rest, K - SPARE, 1)),
        ),
    )
    rows = jnp.where(iota((1, 8, KP), 2) < K, base.reshape(count // 8, 8, KP), tail[None])
    out_ref[...] = rows.reshape(count, KP).astype(BF16)


def result_kernel(recv_ref, code_ref, w_ref, ob_ref, misfit_ref, gram_ref, proj_ref):
    recv = recv_ref[...]
    pick = ones_where(iota((OWN * CAP, REC), 0) == code_ref[...])
    picked = dot(recv, pick, TN)
    values = picked[0:K]
    deeper = jnp.concatenate([picked[1:K], picked[K - 1 : K]], 0)
    weight = w_ref[...]
    misfit_ref[...] = ob_ref[...] - (weight * values + (1.0 - weight) * deeper)
    part = jnp.sum(recv.astype(F32).reshape(OWN * CAP // 8, 8, KP), 0)
    part = part + pltpu.roll(part, 4, 0)
    part = part + pltpu.roll(part, 6, 0)
    sub, line = iota((8, KP), 0), iota((8, KP), 1)
    total = jnp.where(
        line < SPARE,
        pltpu.roll(jnp.broadcast_to(part[0:1], (8, KP)), SPARE, 1),
        pltpu.roll(jnp.broadcast_to(part[1:2], (8, KP)), 2 * SPARE, 1),
    )
    gram = jnp.zeros((8, KP), F32)
    for i, (a, b) in enumerate(PAIRS):
        here = ((sub == a) & (line == b)) | ((sub == b) & (line == a))
        gram = jnp.where(here, total[:, i : i + 1], gram)
    gram_ref[...] = gram[:, 0:MEMBERS]
    proj_ref[...] = pltpu.roll(total, KP - len(PAIRS), 1)[0:1, 0:MEMBERS]


def near(x):
    return pltpu.with_memory_space_constraint(x, VMEM)


def vmem(count):
    return [pl.BlockSpec(memory_space=VMEM)] * count


def smem(count):
    return [pl.BlockSpec(memory_space=SMEM)] * count


def on_device(
    initial_temp, land_mask, pert_table, pert_index, base_kh, member_mix, base_mix,
    owner, column, interp_w, obs_inv_var, observed,
):
    owners = ("lat", "lon")
    mem = lax.axis_index("mem").astype(jnp.int32).reshape(1)
    lat_at, lat_count = lax.axis_index("lat"), lax.axis_size("lat")
    lon_count = lax.axis_size("lon")
    w_t, iv_t, ob_t = interp_w.T, obs_inv_var.T, observed.T

    own_mixes = pl.pallas_call(
        mixes_kernel,
        out_shape=VMEM((4, 2, MIX, KP), BF16),
        in_specs=smem(1) + vmem(2),
        out_specs=vmem(1)[0],
        scratch_shapes=[VMEM((MIX, KP), F32)],
        name="mixes",
    )(pert_index, pert_table, member_mix)
    mixes = lax.all_to_all(own_mixes, "mem", split_axis=0, concat_axis=0, tiled=True)

    cells = jnp.transpose(initial_temp, (1, 2, 0)).astype(BF16)
    cells = jnp.concatenate(
        [
            cells,
            land_mask.astype(BF16)[:, :, None],
            jnp.zeros((CX, CY, KP - K - 1), BF16),
        ],
        2,
    )
    low, top = cells[:, :HALO], cells[:, CY - HALO :]
    even = lat_at % 2 == 0
    inner = [p for i in range(1, lat_count - 1, 2) for p in ((i, i + 1), (i + 1, i))]
    outer = [p for i in range(0, lat_count, 2) for p in ((i, i + 1), (i + 1, i))]
    at_inner = lax.ppermute(jnp.where(even, low, top), "lat", inner)
    at_outer = lax.ppermute(jnp.where(even, top, low), "lat", outer)
    at_inner = jnp.where(lat_at == 0, low[:, ::-1], at_inner)
    at_inner = jnp.where(lat_at == lat_count - 1, top[:, ::-1], at_inner)
    below, above = jnp.where(even, at_inner, at_outer), jnp.where(even, at_outer, at_inner)
    tall = jnp.concatenate([below, cells, above], 1)

    def swap(x, first, by):
        left = [i for i in range(lon_count) if (i // by) % 2 == first]
        pairs = [(i, (i + by) % lon_count) for i in left]
        return lax.ppermute(x, "lon", pairs + [(b, a) for a, b in pairs])

    lon_at = lax.axis_index("lon").astype(jnp.int32).reshape(1)
    second = lon_at[0] // 2 % 2
    first_column, last_column = cells[:1], cells[CX - 1 :]
    near0 = swap(tall, 0, 1)
    near1 = swap(tall, 1, 1)
    far0 = swap(jnp.where(second == 0, last_column, first_column), 0, 2)
    far1 = swap(jnp.where(second == 0, first_column, last_column), 1, 2)

    send, code = pl.pallas_call(
        slots_kernel,
        out_shape=(VMEM((3 * OWN * CAP, KP), BF16), VMEM((1, REC), jnp.int32)),
        in_specs=vmem(5),
        out_specs=tuple(vmem(2)),
        scratch_shapes=[VMEM((3 * KP, REC), F32), VMEM((3 * OWN * CAP, KP), F32)],
        name="slots",
    )(owner.reshape(1, REC), column.reshape(1, REC), w_t, iv_t, ob_t)
    recv = lax.all_to_all(
        send.reshape(OWN, 3, CAP, KP), owners, split_axis=0, concat_axis=0, tiled=True
    )
    recv = recv.reshape(3 * OWN * CAP, KP)

    fields, back = pl.pallas_call(
        functools.partial(window_kernel, scale=1.0 / (OWN * REC * K)),
        out_shape=(VMEM((3, CX, K, CY), BF16), VMEM((OWN * CAP, KP), BF16)),
        in_specs=smem(2) + vmem(9),
        out_specs=tuple(vmem(2)),
        scratch_shapes=[
            VMEM((14, ROWS + 16, KP), F32),
            VMEM((13, CY + 8, KP), F32),
            VMEM((RUNS, 14, ROWS + 16, KP), F32),
            VMEM((RUNS, 14, ROWS + 16, KP), F32),
            VMEM((14, ROWS, KP), F32),
            VMEM((16, KP), F32),
            VMEM((MEMBERS // 2, 2 * KP, 2 * KP), BF16),
            VMEM((2 * KP, 2 * KP), BF16),
            VMEM((KP, 2 * KP), BF16),
            VMEM((3 * OWN * CAP, KP), F32),
            VMEM((MEMBERS, OWN * CAP, KP), F32),
            VMEM((MEMBERS, OWN * CAP, KP), F32),
            VMEM((KP, KP), F32),
        ],
        name="window",
    )(
        mem, lon_at, near(tall), near(near0), near(near1), near(far0), near(far1), near(recv),
        near(mixes),
        base_kh.reshape(1, K), base_mix,
    )

    returned = lax.all_to_all(
        back.reshape(OWN, CAP, KP), owners, split_axis=0, concat_axis=0, tiled=True
    )
    returned = returned.reshape(OWN * CAP, KP)
    misfit_t, gram, proj = pl.pallas_call(
        result_kernel,
        out_shape=(
            jax.ShapeDtypeStruct((K, REC), F32),
            jax.ShapeDtypeStruct((MEMBERS, MEMBERS), F32),
            jax.ShapeDtypeStruct((1, MEMBERS), F32),
        ),
        in_specs=vmem(4),
        out_specs=tuple(vmem(3)),
        name="result",
    )(near(returned), near(code), w_t, ob_t)
    proj = proj.reshape(MEMBERS)
    fields = jnp.transpose(fields, (0, 2, 1, 3))
    member_temp, base_temp = fields[:2], fields[2]

    return member_temp, base_temp, gram, proj, misfit_t.T


def solution(mesh):
    placed = (
        P(None, "lon", "lat"),
        P("lon", "lat"),
        P(),
        P("mem"),
        P(),
        P("mem", None, None),
        P(),
        P(("lat", "lon"), None),
        P(("lat", "lon")),
        P(("lat", "lon"), None),
        P(("lat", "lon"), None),
        P(("lat", "lon"), None),
    )
    return jax.shard_map(
        on_device,
        mesh=mesh,
        in_specs=placed,
        out_specs=(
            P("mem", None, "lon", "lat"),
            P(None, "lon", "lat"),
            P(),
            P(),
            P(("lat", "lon"), None),
        ),
        check_vma=False,
    )
```

profile of v0, /device:TPU:1, one launch (start us, length us, event | category | flops | bytes accessed | tf_op | source)
XLA Modules:
  0.0 98.3 jit_solution(1141098062399458263)
XLA Ops:
  0.6 1.4 %copy.28.mix_ref = bf16[2,100,100]{2,1,0:T(8,128)(2,1)} copy(bf16[2,100,100]{2,0,1:T(2,128)(2,1)} %param.17) | data formatting | bytes 80000 | tf_op args[5]
  2.1 1.6 %mixes.1 = bf16[4,2,104,128]{3,2,1,0:T(8,128)(2,1)} custom-call(s32[2]{0:T(128)} %index_ref.1, f32[16,100]{1,0:T(8,128)} %table_ref.1, bf16[2,100,100]{2,1,0:T(8,128)(2,1)} %copy.28.mix_ref), custom_call_target="tpu_custom_call" | custom-call | tf_op jit(solution)/shard_map/mixes/pallas_call | solution.py:281
  3.6 0.0 copy-start
  3.6 5.0 %all-to-all-start.1 = ((bf16[4,2,104,128]{3,2,1,0:T(8,128)(2,1)}), bf16[4,2,104,128]{3,2,1,0:T(8,128)(2,1)S(1)}, u32[]{:S(2)}, u32[]{:S(2)}) async-start(bf16[4,2,104,128]{3,2,1,0:T(8,128)(2,1)} %mixes.1), calls=%async_computation.1 | async-start | bytes 425984 | tf_op jit(solution)/shard_map/all_to_all | solution.py:289
  8.6 0.0 copy-start.1
  8.6 0.7 copy-done.1
  9.3 0.0 copy-done
  9.3 0.2 copy.26
  9.5 0.2 copy.27
  9.7 0.1 broadcast_select_fusion.5
  9.8 7.3 %collective-permute-start.1 = (bf16[4,8,128]{2,1,0:T(8,128)(2,1)S(1)}, bf16[4,8,128]{2,1,0:T(8,128)(2,1)S(1)}, u32[]{:S(2)}, u32[]{:S(2)}) collective-permute-start(bf16[4,8,128]{2,1,0:T(8,128)(2,1)S(1)} %broadcast_select_fusion.4), channel_id=1, source_target_pairs={{0,32},{32,0},{64,96},{96,64},{1,33},{33,1},{65,97},{97,65},{2,34}... | collective-permute-start | bytes 24584 | tf_op jit(solution)/shard_map/ppermute | solution.py:305
  17.1 2.9 %collective-permute-start = (bf16[4,8,128]{2,1,0:T(8,128)(2,1)S(1)}, bf16[4,8,128]{2,1,0:T(8,128)(2,1)S(1)}, u32[]{:S(2)}, u32[]{:S(2)}) collective-permute-start(bf16[4,8,128]{2,1,0:T(8,128)(2,1)S(1)} %get-tuple-element.39), channel_id=1, source_target_pairs={{32,64},{64,32},{33,65},{65,33},{34,66},{66,34},{35,67},{67,35},{3... | collective-permute-start | bytes 24584 | tf_op jit(solution)/shard_map/ppermute | solution.py:304
  20.1 0.1 broadcast_select_fusion
  20.2 2.3 %slots.1 = (bf16[1536,128]{1,0:T(8,128)(2,1)}, s32[1,256]{1,0:T(1,128)S(1)}) custom-call(s32[1,256]{1,0:T(1,128)} %bitcast.32, s32[1,256]{1,0:T(1,128)} %bitcast.33, f32[100,256]{1,0:T(8,128)} %bitcast.27, f32[100,256]{1,0:T(8,128)} %bitcast.31, f32[100,256]{1,0:T(8,128)} %bitcast.29), custom_call_target="tpu_custom_call" | custom-call | tf_op jit(solution)/shard_map/slots/pallas_call | solution.py:324
  22.5 0.0 all-to-all-done.1.mixes_ref
  22.5 12.2 %all-to-all-start = ((bf16[128,3,4,128]{3,2,1,0:T(4,128)(2,1)}), bf16[128,3,4,128]{3,2,1,0:T(4,128)(2,1)S(1)}, u32[]{:S(2)}, u32[]{:S(2)}) async-start(bf16[128,3,4,128]{3,2,1,0:T(4,128)(2,1)} %bitcast.9), calls=%async_computation | async-start | bytes 786432 | tf_op jit(solution)/shard_map/all_to_all | solution.py:332
  34.7 0.0 collective-permute-done.1
  34.8 0.0 collective-permute-done
  34.8 0.1 pad_maximum_fusion.own_ref
  34.9 7.4 %collective-permute-start.3 = (bf16[4,144,128]{2,1,0:T(8,128)(2,1)S(1)}, bf16[4,144,128]{2,1,0:T(8,128)(2,1)S(1)}, u32[]{:S(2)}, u32[]{:S(2)}) collective-permute-start(bf16[4,144,128]{2,1,0:T(8,128)(2,1)S(1)} %pad_maximum_fusion.own_ref), channel_id=1, source_target_pairs={{1,2},{3,4},{5,6},{7,8},{9,10},{11,12},{13,14},{15,16},{17,18},{19... | collective-permute-start | bytes 442376 | tf_op jit(solution)/shard_map/ppermute | solution.py:314
  42.3 1.9 %collective-permute-start.2 = (bf16[4,144,128]{2,1,0:T(8,128)(2,1)S(1)}, bf16[4,144,128]{2,1,0:T(8,128)(2,1)S(1)}, u32[]{:S(2)}, u32[]{:S(2)}) collective-permute-start(bf16[4,144,128]{2,1,0:T(8,128)(2,1)S(1)} %pad_maximum_fusion.own_ref), channel_id=1, source_target_pairs={{0,1},{2,3},{4,5},{6,7},{8,9},{10,11},{12,13},{14,15},{16,17},{18,... | collective-permute-start | bytes 442376 | tf_op jit(solution)/shard_map/ppermute | solution.py:314
  44.3 1.9 %collective-permute-start.4 = (bf16[1,128,128]{2,1,0:T(8,128)(2,1)S(1)}, bf16[1,128,128]{2,1,0:T(8,128)(2,1)S(1)}, u32[]{:S(2)}, u32[]{:S(2)}) collective-permute-start(bf16[1,128,128]{2,1,0:T(8,128)(2,1)S(1)} %broadcast_select_fusion.1), channel_id=1, source_target_pairs={{0,2},{1,3},{4,6},{5,7},{8,10},{9,11},{12,14},{13,15},{16,18},{17,... | collective-permute-start | bytes 98312 | tf_op jit(solution)/shard_map/ppermute | solution.py:314
  46.2 5.3 %collective-permute-start.5 = (bf16[1,128,128]{2,1,0:T(8,128)(2,1)S(1)}, bf16[1,128,128]{2,1,0:T(8,128)(2,1)S(1)}, u32[]{:S(2)}, u32[]{:S(2)}) collective-permute-start(bf16[1,128,128]{2,1,0:T(8,128)(2,1)S(1)} %get-tuple-element.34), channel_id=1, source_target_pairs={{2,4},{3,5},{6,8},{7,9},{10,12},{11,13},{14,16},{15,17},{18,20},{1... | collective-permute-start | bytes 98312 | tf_op jit(solution)/shard_map/ppermute | solution.py:314
  51.5 1.0 %collective-permute-done.4.far0_ref = bf16[1,128,128]{2,1,0:T(8,128)(2,1)S(1)} collective-permute-done((bf16[1,128,128]{2,1,0:T(8,128)(2,1)S(1)}, bf16[1,128,128]{2,1,0:T(8,128)(2,1)S(1)}, u32[]{:S(2)}, u32[]{:S(2)}) %collective-permute-start.4) | collective-permute-done | bytes 32800 | tf_op jit(solution)/shard_map/ppermute | solution.py:314
  52.6 4.2 %collective-permute-done.5.far1_ref = bf16[1,128,128]{2,1,0:T(8,128)(2,1)S(1)} collective-permute-done((bf16[1,128,128]{2,1,0:T(8,128)(2,1)S(1)}, bf16[1,128,128]{2,1,0:T(8,128)(2,1)S(1)}, u32[]{:S(2)}, u32[]{:S(2)}) %collective-permute-start.5) | collective-permute-done | bytes 32800 | tf_op jit(solution)/shard_map/ppermute | solution.py:314
  56.8 0.0 collective-permute-done.3.near1_ref
  56.8 0.0 collective-permute-done.2.near0_ref
  56.8 0.0 all-to-all-done
  56.8 15.2 %window.1 = (bf16[3,4,100,128]{3,2,1,0:T(8,128)(2,1)S(1)}, bf16[512,128]{1,0:T(8,128)(2,1)}) custom-call(s32[1]{0:T(128)} %bitcast.m_ref, s32[1]{0:T(128)} %bitcast.1.lon_ref, bf16[4,144,128]{2,1,0:T(8,128)(2,1)S(1)} %pad_maximum_fusion.own_ref, bf16[4,144,128]{2,1,0:T(8,128)(2,1)S(1)} %collective-permute-done.2.near0_ref, ...), custom_call_target="tpu_custom_call" | custom-call | tf_op jit(solution)/shard_map/window/pallas_call | solution.py:337
  72.0 10.9 %all-to-all-start.2 = ((bf16[128,4,128]{2,1,0:T(4,128)(2,1)}), bf16[128,4,128]{2,1,0:T(4,128)(2,1)S(1)}, u32[]{:S(2)}, u32[]{:S(2)}) async-start(bf16[128,4,128]{2,1,0:T(4,128)(2,1)} %bitcast.14), calls=%async_computation.2 | async-start | bytes 262144 | tf_op jit(solution)/shard_map/all_to_all | solution.py:364
  82.9 0.8 copy.29
  83.7 0.7 copy.30
  84.4 12.1 %all-to-all-done.2 = bf16[128,4,128]{2,1,0:T(4,128)(2,1)S(1)} async-done(((bf16[128,4,128]{2,1,0:T(4,128)(2,1)}), bf16[128,4,128]{2,1,0:T(4,128)(2,1)S(1)}, u32[]{:S(2)}, u32[]{:S(2)}) %all-to-all-start.2) | async-done | bytes 131104 | tf_op jit(solution)/shard_map/all_to_all | solution.py:364
  96.4 1.8 %result.1 = (f32[100,256]{1,0:T(8,128)}, f32[8,8]{1,0:T(8,128)}, f32[1,8]{1,0:T(1,128)}) custom-call(bf16[512,128]{1,0:T(8,128)(2,1)S(1)} %bitcast.21, s32[1,256]{1,0:T(1,128)S(1)} %get-tuple-element.15.code_ref, f32[100,256]{1,0:T(8,128)} %bitcast.28, f32[100,256]{1,0:T(8,128)} %bitcast.30), custom_call_target="tpu_custom_call" | custom-call | tf_op jit(solution)/shard_map/result/pallas_call | solution.py:368
  (11 shorter events, 0.2 us)
Async XLA Ops:
  3.6 5.7 %copy-start = (f32[100,4,128]{2,1,0:T(4,128)S(1)}, f32[100,4,128]{2,1,0:T(4,128)}, u32[]{:S(2)}) copy-start(f32[100,4,128]{2,1,0:T(4,128)} %param.12) | copy-start | bytes 614404
  3.6 18.9 %all-to-all-start.1 = ((bf16[4,2,104,128]{3,2,1,0:T(8,128)(2,1)}), bf16[4,2,104,128]{3,2,1,0:T(8,128)(2,1)S(1)}, u32[]{:S(2)}, u32[]{:S(2)}) async-start(bf16[4,2,104,128]{3,2,1,0:T(8,128)(2,1)} %mixes.1), calls=%async_computation.1 | async-start | bytes 425984 | tf_op jit(solution)/shard_map/all_to_all | solution.py:289
  8.6 0.7 copy-start.1
  9.8 25.0 %collective-permute-start.1 = (bf16[4,8,128]{2,1,0:T(8,128)(2,1)S(1)}, bf16[4,8,128]{2,1,0:T(8,128)(2,1)S(1)}, u32[]{:S(2)}, u32[]{:S(2)}) collective-permute-start(bf16[4,8,128]{2,1,0:T(8,128)(2,1)S(1)} %broadcast_select_fusion.4), channel_id=1, source_target_pairs={{0,32},{32,0},{64,96},{96,64},{1,33},{33,1},{65,97},{97,65},{2,34}... | collective-permute-start | bytes 24584 | tf_op jit(solution)/shard_map/ppermute | solution.py:305
  17.1 17.6 %collective-permute-start = (bf16[4,8,128]{2,1,0:T(8,128)(2,1)S(1)}, bf16[4,8,128]{2,1,0:T(8,128)(2,1)S(1)}, u32[]{:S(2)}, u32[]{:S(2)}) collective-permute-start(bf16[4,8,128]{2,1,0:T(8,128)(2,1)S(1)} %get-tuple-element.39), channel_id=1, source_target_pairs={{32,64},{64,32},{33,65},{65,33},{34,66},{66,34},{35,67},{67,35},{3... | collective-permute-start | bytes 24584 | tf_op jit(solution)/shard_map/ppermute | solution.py:304
  22.5 34.3 %all-to-all-start = ((bf16[128,3,4,128]{3,2,1,0:T(4,128)(2,1)}), bf16[128,3,4,128]{3,2,1,0:T(4,128)(2,1)S(1)}, u32[]{:S(2)}, u32[]{:S(2)}) async-start(bf16[128,3,4,128]{3,2,1,0:T(4,128)(2,1)} %bitcast.9), calls=%async_computation | async-start | bytes 786432 | tf_op jit(solution)/shard_map/all_to_all | solution.py:332
  34.9 21.9 %collective-permute-start.3 = (bf16[4,144,128]{2,1,0:T(8,128)(2,1)S(1)}, bf16[4,144,128]{2,1,0:T(8,128)(2,1)S(1)}, u32[]{:S(2)}, u32[]{:S(2)}) collective-permute-start(bf16[4,144,128]{2,1,0:T(8,128)(2,1)S(1)} %pad_maximum_fusion.own_ref), channel_id=1, source_target_pairs={{1,2},{3,4},{5,6},{7,8},{9,10},{11,12},{13,14},{15,16},{17,18},{19... | collective-permute-start | bytes 442376 | tf_op jit(solution)/shard_map/ppermute | solution.py:314
  42.3 14.5 %collective-permute-start.2 = (bf16[4,144,128]{2,1,0:T(8,128)(2,1)S(1)}, bf16[4,144,128]{2,1,0:T(8,128)(2,1)S(1)}, u32[]{:S(2)}, u32[]{:S(2)}) collective-permute-start(bf16[4,144,128]{2,1,0:T(8,128)(2,1)S(1)} %pad_maximum_fusion.own_ref), channel_id=1, source_target_pairs={{0,1},{2,3},{4,5},{6,7},{8,9},{10,11},{12,13},{14,15},{16,17},{18,... | collective-permute-start | bytes 442376 | tf_op jit(solution)/shard_map/ppermute | solution.py:314
  44.3 8.3 %collective-permute-start.4 = (bf16[1,128,128]{2,1,0:T(8,128)(2,1)S(1)}, bf16[1,128,128]{2,1,0:T(8,128)(2,1)S(1)}, u32[]{:S(2)}, u32[]{:S(2)}) collective-permute-start(bf16[1,128,128]{2,1,0:T(8,128)(2,1)S(1)} %broadcast_select_fusion.1), channel_id=1, source_target_pairs={{0,2},{1,3},{4,6},{5,7},{8,10},{9,11},{12,14},{13,15},{16,18},{17,... | collective-permute-start | bytes 98312 | tf_op jit(solution)/shard_map/ppermute | solution.py:314
  46.2 10.6 %collective-permute-start.5 = (bf16[1,128,128]{2,1,0:T(8,128)(2,1)S(1)}, bf16[1,128,128]{2,1,0:T(8,128)(2,1)S(1)}, u32[]{:S(2)}, u32[]{:S(2)}) collective-permute-start(bf16[1,128,128]{2,1,0:T(8,128)(2,1)S(1)} %get-tuple-element.34), channel_id=1, source_target_pairs={{2,4},{3,5},{6,8},{7,9},{10,12},{11,13},{14,16},{15,17},{18,20},{1... | collective-permute-start | bytes 98312 | tf_op jit(solution)/shard_map/ppermute | solution.py:314
  72.0 24.5 %all-to-all-start.2 = ((bf16[128,4,128]{2,1,0:T(4,128)(2,1)}), bf16[128,4,128]{2,1,0:T(4,128)(2,1)S(1)}, u32[]{:S(2)}, u32[]{:S(2)}) async-start(bf16[128,4,128]{2,1,0:T(4,128)(2,1)} %bitcast.14), calls=%async_computation.2 | async-start | bytes 262144 | tf_op jit(solution)/shard_map/all_to_all | solution.py:364
where the time goes:
time: 99 us; the launch traced here: 98.3 us
  starting transfers between devices  54.9 us (55%)
  Pallas kernels  20.8 us (21%)
  waiting for transfers between devices  17.3 us (17%)
  local copies, waits for them, and re-layouts  3.99 us (4%)
    ppermute x4, starting transfers between devices, swap(): return lax.ppermute(x, 'lon', pairs + [(b, a) for a, b in pairs])  16.5 us
    pallas_call x1, Pallas kernels, on_device(): pl.pallas_call(functools.partial(window_kernel, scale=1.0 / (OWN * REC *...  15.2 us
    all_to_all x1, starting transfers between devices, on_device(): lax.all_to_all(send.reshape(OWN, 3, CAP, KP), owners, split_axis=0, conca...  12.2 us
    all_to_all x1, waiting for transfers between devices, on_device(): lax.all_to_all(back.reshape(OWN, CAP, KP), owners, split_axis=0, concat_a...  12.1 us
    all_to_all x1, starting transfers between devices, on_device(): lax.all_to_all(back.reshape(OWN, CAP, KP), owners, split_axis=0, concat_a...  10.9 us
    ppermute x1, starting transfers between devices, on_device(): at_outer = lax.ppermute(jnp.where(even, top, low), 'lat', outer)  7.31 us
    ppermute x4, waiting for transfers between devices, swap(): return lax.ppermute(x, 'lon', pairs + [(b, a) for a, b in pairs])  5.27 us
    all_to_all x1, starting transfers between devices, on_device(): lax.all_to_all(own_mixes, 'mem', split_axis=0, concat_axis=0, tiled=True)  4.96 us
  transfers between devices with their start and end apart: 9, of which 3 were waited for; matrix products, arithmetic and copies ran while one was open for 2% of the time, Pallas kernels for 2%

commit v1 on v0

--- a/solution.py
+++ b/solution.py
@@ -78,6 +78,27 @@
         packed = pad[...].astype(BF16)
         for copy in range(4):
             out_ref[copy, j] = packed
+
+
+def cells_kernel(
+    lat_ref, lon_ref, temp_ref, mask_ref,
+    cells_ref, inner_ref, outer_ref, far0_ref, far1_ref, pad,
+):
+    even = lax.rem(lat_ref[0], 2) == 0
+    second = lax.rem(lon_ref[0] // 2, 2) == 0
+    pad[...] = jnp.zeros((KP, CY), F32)
+    turned = []
+    for c in range(CX):
+        pad[0:K, :] = temp_ref[:, c, :]
+        pad[K : K + 1, :] = mask_ref[c : c + 1, :].astype(F32)
+        x = pad[...].T
+        low, top = x[0:HALO], x[CY - HALO : CY]
+        cells_ref[c] = x.astype(BF16)
+        inner_ref[c] = jnp.where(even, low, top).astype(BF16)
+        outer_ref[c] = jnp.where(even, top, low).astype(BF16)
+        turned.append(x)
+    far0_ref[0] = jnp.where(second, turned[-1], turned[0]).astype(BF16)
+    far1_ref[0] = jnp.where(second, turned[0], turned[-1]).astype(BF16)
 
 
 def window_kernel(
@@ -288,21 +309,28 @@
     )(pert_index, pert_table, member_mix)
     mixes = lax.all_to_all(own_mixes, "mem", split_axis=0, concat_axis=0, tiled=True)
 
-    cells = jnp.transpose(initial_temp, (1, 2, 0)).astype(BF16)
-    cells = jnp.concatenate(
-        [
-            cells,
-            land_mask.astype(BF16)[:, :, None],
-            jnp.zeros((CX, CY, KP - K - 1), BF16),
-        ],
-        2,
-    )
+    lat_row = lat_at.astype(jnp.int32).reshape(1)
+    lon_at = lax.axis_index("lon").astype(jnp.int32).reshape(1)
+    cells, for_inner, for_outer, for_far0, for_far1 = pl.pallas_call(
+        cells_kernel,
+        out_shape=(
+            VMEM((CX, CY, KP), BF16),
+            VMEM((CX, HALO, KP), BF16),
+            VMEM((CX, HALO, KP), BF16),
+            VMEM((1, CY, KP), BF16),
+            VMEM((1, CY, KP), BF16),
+        ),
+        in_specs=smem(2) + vmem(2),
+        out_specs=tuple(vmem(5)),
+        scratch_shapes=[VMEM((KP, CY), F32)],
+        name="cells",
+    )(lat_row, lon_at, near(initial_temp), near(land_mask))
     low, top = cells[:, :HALO], cells[:, CY - HALO :]
     even = lat_at % 2 == 0
     inner = [p for i in range(1, lat_count - 1, 2) for p in ((i, i + 1), (i + 1, i))]
     outer = [p for i in range(0, lat_count, 2) for p in ((i, i + 1), (i + 1, i))]
-    at_inner = lax.ppermute(jnp.where(even, low, top), "lat", inner)
-    at_outer = lax.ppermute(jnp.where(even, top, low), "lat", outer)
+    at_inner = lax.ppermute(for_inner, "lat", inner)
+    at_outer = lax.ppermute(for_outer, "lat", outer)
     at_inner = jnp.where(lat_at == 0, low[:, ::-1], at_inner)
     at_inner = jnp.where(lat_at == lat_count - 1, top[:, ::-1], at_inner)
     below, above = jnp.where(even, at_inner, at_outer), jnp.where(even, at_outer, at_inner)
@@ -313,13 +341,10 @@
         pairs = [(i, (i + by) % lon_count) for i in left]
         return lax.ppermute(x, "lon", pairs + [(b, a) for a, b in pairs])
 
-    lon_at = lax.axis_index("lon").astype(jnp.int32).reshape(1)
-    second = lon_at[0] // 2 % 2
-    first_column, last_column = cells[:1], cells[CX - 1 :]
     near0 = swap(tall, 0, 1)
     near1 = swap(tall, 1, 1)
-    far0 = swap(jnp.where(second == 0, last_column, first_column), 0, 2)
-    far1 = swap(jnp.where(second == 0, first_column, last_column), 1, 2)
+    far0 = swap(for_far0, 0, 2)
+    far1 = swap(for_far1, 1, 2)
 
     send, code = pl.pallas_call(
         slots_kernel,
@@ -328,7 +353,7 @@
         out_specs=tuple(vmem(2)),
         scratch_shapes=[VMEM((3 * KP, REC), F32), VMEM((3 * OWN * CAP, KP), F32)],
         name="slots",
-    )(owner.reshape(1, REC), column.reshape(1, REC), w_t, iv_t, ob_t)
+    )(owner.reshape(1, REC), column.reshape(1, REC), near(w_t), near(iv_t), near(ob_t))
     recv = lax.all_to_all(
         send.reshape(OWN, 3, CAP, KP), owners, split_axis=0, concat_axis=0, tiled=True
     )
@@ -375,7 +400,7 @@
         in_specs=vmem(4),
         out_specs=tuple(vmem(3)),
         name="result",
-    )(near(returned), near(code), w_t, ob_t)
+    )(near(returned), near(code), near(w_t), near(ob_t))
     proj = proj.reshape(MEMBERS)
     fields = jnp.transpose(fields, (0, 2, 1, 3))
     member_temp, base_temp = fields[:2], fields[2]

time: 99 us -> 97.5 us (0.985)
  Pallas kernels: 20.8 us -> 19.8 us
    unnamed x7 -> x13, local copies, waits for them, and re-layouts: 3.56 us -> 3.57 us
where the time goes in v1:
time: 97.5 us; the launch traced here: 96.8 us
  starting transfers between devices  55 us (56%)
  Pallas kernels  19.8 us (20%)
  waiting for transfers between devices  17.6 us (18%)
  local copies, waits for them, and re-layouts  3.64 us (4%)
    ppermute x4, starting transfers between devices, swap(): return lax.ppermute(x, 'lon', pairs + [(b, a) for a, b in pairs])  16.4 us
    pallas_call x1, Pallas kernels, on_device(): pl.pallas_call(functools.partial(window_kernel, scale=1.0 / (OWN * REC *...  15.2 us
    all_to_all x1, starting transfers between devices, on_device(): lax.all_to_all(send.reshape(OWN, 3, CAP, KP), owners, split_axis=0, conca...  12.6 us
    all_to_all x1, waiting for transfers between devices, on_device(): lax.all_to_all(back.reshape(OWN, CAP, KP), owners, split_axis=0, concat_a...  12.1 us
    all_to_all x1, starting transfers between devices, on_device(): lax.all_to_all(back.reshape(OWN, CAP, KP), owners, split_axis=0, concat_a...  10.9 us
    ppermute x1, starting transfers between devices, on_device(): at_inner = lax.ppermute(for_inner, 'lat', inner)  8.29 us
    ppermute x4, waiting for transfers between devices, swap(): return lax.ppermute(x, 'lon', pairs + [(b, a) for a, b in pairs])  5.53 us
    all_to_all x1, starting transfers between devices, on_device(): lax.all_to_all(own_mixes, 'mem', split_axis=0, concat_axis=0, tiled=True)  4.96 us
  transfers between devices with their start and end apart: 9, of which 3 were waited for; matrix products, arithmetic and copies ran while one was open for 2% of the time, Pallas kernels for 2%

profile of v1, /device:TPU:1, one launch (start us, length us, event | category | flops | bytes accessed | tf_op | source)
XLA Modules:
  0.0 96.8 jit_solution(4719066882258261320)
XLA Ops:
  0.6 1.4 %copy.17.mix_ref = bf16[2,100,100]{2,1,0:T(8,128)(2,1)} copy(bf16[2,100,100]{2,0,1:T(2,128)(2,1)} %param.17) | data formatting | bytes 80000 | tf_op args[5]
  2.1 1.6 %mixes.1 = bf16[4,2,104,128]{3,2,1,0:T(8,128)(2,1)} custom-call(s32[2]{0:T(128)} %index_ref.1, f32[16,100]{1,0:T(8,128)} %table_ref.1, bf16[2,100,100]{2,1,0:T(8,128)(2,1)} %copy.17.mix_ref), custom_call_target="tpu_custom_call" | custom-call | tf_op jit(solution)/shard_map/mixes/pallas_call | solution.py:302
  3.6 0.0 copy-start.2
  3.6 0.0 copy-start.3
  3.6 5.0 %all-to-all-start.1 = ((bf16[4,2,104,128]{3,2,1,0:T(8,128)(2,1)}), bf16[4,2,104,128]{3,2,1,0:T(8,128)(2,1)S(1)}, u32[]{:S(2)}, u32[]{:S(2)}) async-start(bf16[4,2,104,128]{3,2,1,0:T(8,128)(2,1)} %mixes.1), calls=%async_computation.1 | async-start | bytes 425984 | tf_op jit(solution)/shard_map/all_to_all | solution.py:310
  8.6 0.0 copy-start.4
  8.6 0.0 copy-done.2
  8.6 0.7 copy-done.4
  9.3 0.0 copy-start
  9.3 0.0 copy-start.1
  9.3 0.2 cells.1
  9.5 8.3 %collective-permute-start = (bf16[4,8,128]{2,1,0:T(8,128)(2,1)S(1)}, bf16[4,8,128]{2,1,0:T(8,128)(2,1)S(1)}, u32[]{:S(2)}, u32[]{:S(2)}) collective-permute-start(bf16[4,8,128]{2,1,0:T(8,128)(2,1)S(1)} %get-tuple-element.18), channel_id=1, source_target_pairs={{32,64},{64,32},{33,65},{65,33},{34,66},{66,34},{35,67},{67,35},{3... | collective-permute-start | bytes 24584 | tf_op jit(solution)/shard_map/ppermute | solution.py:332
  17.8 1.9 %collective-permute-start.1 = (bf16[4,8,128]{2,1,0:T(8,128)(2,1)S(1)}, bf16[4,8,128]{2,1,0:T(8,128)(2,1)S(1)}, u32[]{:S(2)}, u32[]{:S(2)}) collective-permute-start(bf16[4,8,128]{2,1,0:T(8,128)(2,1)S(1)} %get-tuple-element.19), channel_id=1, source_target_pairs={{0,32},{32,0},{64,96},{96,64},{1,33},{33,1},{65,97},{97,65},{2,34}... | collective-permute-start | bytes 24584 | tf_op jit(solution)/shard_map/ppermute | solution.py:333
  19.7 0.0 copy-done.3
  19.7 0.0 copy-done
  19.7 0.0 copy-done.1
  19.7 2.0 %slots.1 = (bf16[1536,128]{1,0:T(8,128)(2,1)}, s32[1,256]{1,0:T(1,128)S(1)}) custom-call(s32[1,256]{1,0:T(1,128)} %bitcast.27, s32[1,256]{1,0:T(1,128)} %bitcast.28, f32[100,256]{1,0:T(8,128)S(1)} %bitcast.20, f32[100,256]{1,0:T(8,128)S(1)} %bitcast.26, f32[100,256]{1,0:T(8,128)S(1)} %bitcast.22), custom_call_target="tpu_custom_call" | custom-call | tf_op jit(solution)/shard_map/slots/pallas_call | solution.py:349
  21.7 0.0 all-to-all-done.1.mixes_ref
  21.7 12.6 %all-to-all-start = ((bf16[128,3,4,128]{3,2,1,0:T(4,128)(2,1)}), bf16[128,3,4,128]{3,2,1,0:T(4,128)(2,1)S(1)}, u32[]{:S(2)}, u32[]{:S(2)}) async-start(bf16[128,3,4,128]{3,2,1,0:T(4,128)(2,1)} %bitcast.8), calls=%async_computation | async-start | bytes 786432 | tf_op jit(solution)/shard_map/all_to_all | solution.py:357
  34.4 0.0 collective-permute-done
  34.4 0.0 collective-permute-done.1
  34.4 7.4 %collective-permute-start.3 = (bf16[4,144,128]{2,1,0:T(8,128)(2,1)S(1)}, bf16[4,144,128]{2,1,0:T(8,128)(2,1)S(1)}, u32[]{:S(2)}, u32[]{:S(2)}) collective-permute-start(bf16[4,144,128]{2,1,0:T(8,128)(2,1)S(1)} %pad_maximum_fusion.own_ref), channel_id=1, source_target_pairs={{1,2},{3,4},{5,6},{7,8},{9,10},{11,12},{13,14},{15,16},{17,18},{19... | collective-permute-start | bytes 442376 | tf_op jit(solution)/shard_map/ppermute | solution.py:342
  41.8 1.9 %collective-permute-start.2 = (bf16[4,144,128]{2,1,0:T(8,128)(2,1)S(1)}, bf16[4,144,128]{2,1,0:T(8,128)(2,1)S(1)}, u32[]{:S(2)}, u32[]{:S(2)}) collective-permute-start(bf16[4,144,128]{2,1,0:T(8,128)(2,1)S(1)} %pad_maximum_fusion.own_ref), channel_id=1, source_target_pairs={{0,1},{2,3},{4,5},{6,7},{8,9},{10,11},{12,13},{14,15},{16,17},{18,... | collective-permute-start | bytes 442376 | tf_op jit(solution)/shard_map/ppermute | solution.py:342
  43.8 1.9 %collective-permute-start.4 = (bf16[1,128,128]{2,1,0:T(8,128)(2,1)S(1)}, bf16[1,128,128]{2,1,0:T(8,128)(2,1)S(1)}, u32[]{:S(2)}, u32[]{:S(2)}) collective-permute-start(bf16[1,128,128]{2,1,0:T(8,128)(2,1)S(1)} %get-tuple-element.20), channel_id=1, source_target_pairs={{0,2},{1,3},{4,6},{5,7},{8,10},{9,11},{12,14},{13,15},{16,18},{17,... | collective-permute-start | bytes 98312 | tf_op jit(solution)/shard_map/ppermute | solution.py:342
  45.7 5.1 %collective-permute-start.5 = (bf16[1,128,128]{2,1,0:T(8,128)(2,1)S(1)}, bf16[1,128,128]{2,1,0:T(8,128)(2,1)S(1)}, u32[]{:S(2)}, u32[]{:S(2)}) collective-permute-start(bf16[1,128,128]{2,1,0:T(8,128)(2,1)S(1)} %get-tuple-element.21), channel_id=1, source_target_pairs={{2,4},{3,5},{6,8},{7,9},{10,12},{11,13},{14,16},{15,17},{18,20},{1... | collective-permute-start | bytes 98312 | tf_op jit(solution)/shard_map/ppermute | solution.py:342
  50.8 1.3 %collective-permute-done.4.far0_ref = bf16[1,128,128]{2,1,0:T(8,128)(2,1)S(1)} collective-permute-done((bf16[1,128,128]{2,1,0:T(8,128)(2,1)S(1)}, bf16[1,128,128]{2,1,0:T(8,128)(2,1)S(1)}, u32[]{:S(2)}, u32[]{:S(2)}) %collective-permute-start.4) | collective-permute-done | bytes 32800 | tf_op jit(solution)/shard_map/ppermute | solution.py:342
  52.1 4.2 %collective-permute-done.5.far1_ref = bf16[1,128,128]{2,1,0:T(8,128)(2,1)S(1)} collective-permute-done((bf16[1,128,128]{2,1,0:T(8,128)(2,1)S(1)}, bf16[1,128,128]{2,1,0:T(8,128)(2,1)S(1)}, u32[]{:S(2)}, u32[]{:S(2)}) %collective-permute-start.5) | collective-permute-done | bytes 32800 | tf_op jit(solution)/shard_map/ppermute | solution.py:342
  56.4 0.0 collective-permute-done.3.near1_ref
  56.4 0.0 collective-permute-done.2.near0_ref
  56.4 0.0 all-to-all-done
  56.4 15.2 %window.1 = (bf16[3,4,100,128]{3,2,1,0:T(8,128)(2,1)S(1)}, bf16[512,128]{1,0:T(8,128)(2,1)}) custom-call(s32[1]{0:T(128)} %bitcast.m_ref, s32[1]{0:T(128)} %bitcast.1.lon_ref, bf16[4,144,128]{2,1,0:T(8,128)(2,1)S(1)} %pad_maximum_fusion.own_ref, bf16[4,144,128]{2,1,0:T(8,128)(2,1)S(1)} %collective-permute-done.2.near0_ref, ...), custom_call_target="tpu_custom_call" | custom-call | tf_op jit(solution)/shard_map/window/pallas_call | solution.py:362
  71.5 10.9 %all-to-all-start.2 = ((bf16[128,4,128]{2,1,0:T(4,128)(2,1)}), bf16[128,4,128]{2,1,0:T(4,128)(2,1)S(1)}, u32[]{:S(2)}, u32[]{:S(2)}) async-start(bf16[128,4,128]{2,1,0:T(4,128)(2,1)} %bitcast.13), calls=%async_computation.2 | async-start | bytes 262144 | tf_op jit(solution)/shard_map/all_to_all | solution.py:389
  82.4 0.8 copy.18
  83.2 0.7 copy.19
  83.9 12.1 %all-to-all-done.2 = bf16[128,4,128]{2,1,0:T(4,128)(2,1)S(1)} async-done(((bf16[128,4,128]{2,1,0:T(4,128)(2,1)}), bf16[128,4,128]{2,1,0:T(4,128)(2,1)S(1)}, u32[]{:S(2)}, u32[]{:S(2)}) %all-to-all-start.2) | async-done | bytes 131104 | tf_op jit(solution)/shard_map/all_to_all | solution.py:389
  95.9 0.9 result.1
  (8 shorter events, 0.1 us)
Async XLA Ops:
  3.6 5.0 %copy-start.2 = (f32[100,4,128]{2,1,0:T(4,128)S(1)}, f32[100,4,128]{2,1,0:T(4,128)}, u32[]{:S(2)}) copy-start(f32[100,4,128]{2,1,0:T(4,128)} %temp_ref.1) | copy-start | bytes 614404
  3.6 16.1 %copy-start.3 = (f32[256,100]{0,1:T(8,128)S(1)}, f32[256,100]{0,1:T(8,128)}, u32[]{:S(2)}) copy-start(f32[256,100]{0,1:T(8,128)} %param.22) | copy-start | bytes 307204
  3.6 18.1 %all-to-all-start.1 = ((bf16[4,2,104,128]{3,2,1,0:T(8,128)(2,1)}), bf16[4,2,104,128]{3,2,1,0:T(8,128)(2,1)S(1)}, u32[]{:S(2)}, u32[]{:S(2)}) async-start(bf16[4,2,104,128]{3,2,1,0:T(8,128)(2,1)} %mixes.1), calls=%async_computation.1 | async-start | bytes 425984 | tf_op jit(solution)/shard_map/all_to_all | solution.py:310
  8.6 0.7 copy-start.4
  9.3 10.4 %copy-start = (f32[256,100]{0,1:T(8,128)S(1)}, f32[256,100]{0,1:T(8,128)}, u32[]{:S(2)}) copy-start(f32[256,100]{0,1:T(8,128)} %param.21) | copy-start | bytes 307204
  9.3 10.5 %copy-start.1 = (f32[256,100]{0,1:T(8,128)S(1)}, f32[256,100]{0,1:T(8,128)}, u32[]{:S(2)}) copy-start(f32[256,100]{0,1:T(8,128)} %param.23) | copy-start | bytes 307204
  9.5 24.9 %collective-permute-start = (bf16[4,8,128]{2,1,0:T(8,128)(2,1)S(1)}, bf16[4,8,128]{2,1,0:T(8,128)(2,1)S(1)}, u32[]{:S(2)}, u32[]{:S(2)}) collective-permute-start(bf16[4,8,128]{2,1,0:T(8,128)(2,1)S(1)} %get-tuple-element.18), channel_id=1, source_target_pairs={{32,64},{64,32},{33,65},{65,33},{34,66},{66,34},{35,67},{67,35},{3... | collective-permute-start | bytes 24584 | tf_op jit(solution)/shard_map/ppermute | solution.py:332
  17.8 16.6 %collective-permute-start.1 = (bf16[4,8,128]{2,1,0:T(8,128)(2,1)S(1)}, bf16[4,8,128]{2,1,0:T(8,128)(2,1)S(1)}, u32[]{:S(2)}, u32[]{:S(2)}) collective-permute-start(bf16[4,8,128]{2,1,0:T(8,128)(2,1)S(1)} %get-tuple-element.19), channel_id=1, source_target_pairs={{0,32},{32,0},{64,96},{96,64},{1,33},{33,1},{65,97},{97,65},{2,34}... | collective-permute-start | bytes 24584 | tf_op jit(solution)/shard_map/ppermute | solution.py:333
  21.7 34.6 %all-to-all-start = ((bf16[128,3,4,128]{3,2,1,0:T(4,128)(2,1)}), bf16[128,3,4,128]{3,2,1,0:T(4,128)(2,1)S(1)}, u32[]{:S(2)}, u32[]{:S(2)}) async-start(bf16[128,3,4,128]{3,2,1,0:T(4,128)(2,1)} %bitcast.8), calls=%async_computation | async-start | bytes 786432 | tf_op jit(solution)/shard_map/all_to_all | solution.py:357
  34.4 21.9 %collective-permute-start.3 = (bf16[4,144,128]{2,1,0:T(8,128)(2,1)S(1)}, bf16[4,144,128]{2,1,0:T(8,128)(2,1)S(1)}, u32[]{:S(2)}, u32[]{:S(2)}) collective-permute-start(bf16[4,144,128]{2,1,0:T(8,128)(2,1)S(1)} %pad_maximum_fusion.own_ref), channel_id=1, source_target_pairs={{1,2},{3,4},{5,6},{7,8},{9,10},{11,12},{13,14},{15,16},{17,18},{19... | collective-permute-start | bytes 442376 | tf_op jit(solution)/shard_map/ppermute | solution.py:342
  41.8 14.5 %collective-permute-start.2 = (bf16[4,144,128]{2,1,0:T(8,128)(2,1)S(1)}, bf16[4,144,128]{2,1,0:T(8,128)(2,1)S(1)}, u32[]{:S(2)}, u32[]{:S(2)}) collective-permute-start(bf16[4,144,128]{2,1,0:T(8,128)(2,1)S(1)} %pad_maximum_fusion.own_ref), channel_id=1, source_target_pairs={{0,1},{2,3},{4,5},{6,7},{8,9},{10,11},{12,13},{14,15},{16,17},{18,... | collective-permute-start | bytes 442376 | tf_op jit(solution)/shard_map/ppermute | solution.py:342
  43.8 8.4 %collective-permute-start.4 = (bf16[1,128,128]{2,1,0:T(8,128)(2,1)S(1)}, bf16[1,128,128]{2,1,0:T(8,128)(2,1)S(1)}, u32[]{:S(2)}, u32[]{:S(2)}) collective-permute-start(bf16[1,128,128]{2,1,0:T(8,128)(2,1)S(1)} %get-tuple-element.20), channel_id=1, source_target_pairs={{0,2},{1,3},{4,6},{5,7},{8,10},{9,11},{12,14},{13,15},{16,18},{17,... | collective-permute-start | bytes 98312 | tf_op jit(solution)/shard_map/ppermute | solution.py:342
  45.7 10.7 %collective-permute-start.5 = (bf16[1,128,128]{2,1,0:T(8,128)(2,1)S(1)}, bf16[1,128,128]{2,1,0:T(8,128)(2,1)S(1)}, u32[]{:S(2)}, u32[]{:S(2)}) collective-permute-start(bf16[1,128,128]{2,1,0:T(8,128)(2,1)S(1)} %get-tuple-element.21), channel_id=1, source_target_pairs={{2,4},{3,5},{6,8},{7,9},{10,12},{11,13},{14,16},{15,17},{18,20},{1... | collective-permute-start | bytes 98312 | tf_op jit(solution)/shard_map/ppermute | solution.py:342
  71.5 24.4 %all-to-all-start.2 = ((bf16[128,4,128]{2,1,0:T(4,128)(2,1)}), bf16[128,4,128]{2,1,0:T(4,128)(2,1)S(1)}, u32[]{:S(2)}, u32[]{:S(2)}) async-start(bf16[128,4,128]{2,1,0:T(4,128)(2,1)} %bitcast.13), calls=%async_computation.2 | async-start | bytes 262144 | tf_op jit(solution)/shard_map/all_to_all | solution.py:389

commit v2 on v1

--- a/solution.py
+++ b/solution.py
@@ -68,9 +68,10 @@
 
 
 def mixes_kernel(index_ref, table_ref, mix_ref, out_ref, pad):
+    pair = mix_ref[...].astype(F32)
     for j in range(2):
         pad[...] = jnp.zeros((MIX, KP), F32)
-        pad[0:K, 0:K] = mix_ref[j].astype(F32)
+        pad[0:K, 0:K] = pair[:, j, :]
         kh = table_ref[pl.ds(index_ref[j], 1), :]
         high = kh.astype(BF16).astype(F32)
         pad[K : K + 1, 0:K] = high
@@ -306,7 +307,7 @@
         out_specs=vmem(1)[0],
         scratch_shapes=[VMEM((MIX, KP), F32)],
         name="mixes",
-    )(pert_index, pert_table, member_mix)
+    )(pert_index, pert_table, jnp.transpose(member_mix, (1, 0, 2)))
     mixes = lax.all_to_all(own_mixes, "mem", split_axis=0, concat_axis=0, tiled=True)
 
     lat_row = lat_at.astype(jnp.int32).reshape(1)

time: 97.5 us -> 96.1 us (0.986)
  local copies, waits for them, and re-layouts: 3.64 us -> 2.21 us
    unnamed x13 -> x12, local copies, waits for them, and re-layouts: 3.57 us -> 2.13 us
where the time goes in v2:
time: 96.1 us; the launch traced here: 95.5 us
  starting transfers between devices  55 us (57%)
  Pallas kernels  19.9 us (21%)
  waiting for transfers between devices  17.6 us (18%)
  local copies, waits for them, and re-layouts  2.21 us (2%)
    ppermute x4, starting transfers between devices, swap(): return lax.ppermute(x, 'lon', pairs + [(b, a) for a, b in pairs])  16.4 us
    pallas_call x1, Pallas kernels, on_device(): pl.pallas_call(functools.partial(window_kernel, scale=1.0 / (OWN * REC *...  15.2 us
    all_to_all x1, starting transfers between devices, on_device(): lax.all_to_all(send.reshape(OWN, 3, CAP, KP), owners, split_axis=0, conca...  12.6 us
    all_to_all x1, waiting for transfers between devices, on_device(): lax.all_to_all(back.reshape(OWN, CAP, KP), owners, split_axis=0, concat_a...  12.1 us
    all_to_all x1, starting transfers between devices, on_device(): lax.all_to_all(back.reshape(OWN, CAP, KP), owners, split_axis=0, concat_a...  10.9 us
    ppermute x1, starting transfers between devices, on_device(): at_inner = lax.ppermute(for_inner, 'lat', inner)  8.29 us
    ppermute x4, waiting for transfers between devices, swap(): return lax.ppermute(x, 'lon', pairs + [(b, a) for a, b in pairs])  5.53 us
    all_to_all x1, starting transfers between devices, on_device(): lax.all_to_all(own_mixes, 'mem', split_axis=0, concat_axis=0, tiled=True)  4.96 us
  transfers between devices with their start and end apart: 9, of which 3 were waited for; matrix products, arithmetic and copies ran while one was open for 2% of the time, Pallas kernels for 2%

profile of v2, /device:TPU:1, one launch (start us, length us, event | category | flops | bytes accessed | tf_op | source)
XLA Modules:
  0.0 95.5 jit_solution(732957574445523365)
XLA Ops:
  0.6 1.7 %mixes.1 = bf16[4,2,104,128]{3,2,1,0:T(8,128)(2,1)} custom-call(s32[2]{0:T(128)} %index_ref.1, f32[16,100]{1,0:T(8,128)} %table_ref.1, bf16[100,2,100]{2,1,0:T(2,128)(2,1)} %bitcast.28), custom_call_target="tpu_custom_call" | custom-call | tf_op jit(solution)/shard_map/mixes/pallas_call | solution.py:303
  2.3 0.0 copy-start.2
  2.3 0.0 copy-start.3
  2.3 5.0 %all-to-all-start.1 = ((bf16[4,2,104,128]{3,2,1,0:T(8,128)(2,1)}), bf16[4,2,104,128]{3,2,1,0:T(8,128)(2,1)S(1)}, u32[]{:S(2)}, u32[]{:S(2)}) async-start(bf16[4,2,104,128]{3,2,1,0:T(8,128)(2,1)} %mixes.1), calls=%async_computation.1 | async-start | bytes 425984 | tf_op jit(solution)/shard_map/all_to_all | solution.py:311
  7.3 0.0 copy-start.4
  7.3 0.0 copy-done.2
  7.3 0.7 copy-done.4
  7.9 0.0 copy-start
  7.9 0.0 copy-start.1
  7.9 0.2 cells.1
  8.1 8.3 %collective-permute-start = (bf16[4,8,128]{2,1,0:T(8,128)(2,1)S(1)}, bf16[4,8,128]{2,1,0:T(8,128)(2,1)S(1)}, u32[]{:S(2)}, u32[]{:S(2)}) collective-permute-start(bf16[4,8,128]{2,1,0:T(8,128)(2,1)S(1)} %get-tuple-element.18), channel_id=1, source_target_pairs={{32,64},{64,32},{33,65},{65,33},{34,66},{66,34},{35,67},{67,35},{3... | collective-permute-start | bytes 24584 | tf_op jit(solution)/shard_map/ppermute | solution.py:333
  16.4 1.9 %collective-permute-start.1 = (bf16[4,8,128]{2,1,0:T(8,128)(2,1)S(1)}, bf16[4,8,128]{2,1,0:T(8,128)(2,1)S(1)}, u32[]{:S(2)}, u32[]{:S(2)}) collective-permute-start(bf16[4,8,128]{2,1,0:T(8,128)(2,1)S(1)} %get-tuple-element.19), channel_id=1, source_target_pairs={{0,32},{32,0},{64,96},{96,64},{1,33},{33,1},{65,97},{97,65},{2,34}... | collective-permute-start | bytes 24584 | tf_op jit(solution)/shard_map/ppermute | solution.py:334
  18.4 0.0 copy-done.3
  18.4 0.0 copy-done
  18.4 0.0 copy-done.1
  18.4 2.0 %slots.1 = (bf16[1536,128]{1,0:T(8,128)(2,1)}, s32[1,256]{1,0:T(1,128)S(1)}) custom-call(s32[1,256]{1,0:T(1,128)} %bitcast.29, s32[1,256]{1,0:T(1,128)} %bitcast.30, f32[100,256]{1,0:T(8,128)S(1)} %bitcast.21, f32[100,256]{1,0:T(8,128)S(1)} %bitcast.27, f32[100,256]{1,0:T(8,128)S(1)} %bitcast.23), custom_call_target="tpu_custom_call" | custom-call | tf_op jit(solution)/shard_map/slots/pallas_call | solution.py:350
  20.4 0.0 all-to-all-done.1.mixes_ref
  20.4 12.6 %all-to-all-start = ((bf16[128,3,4,128]{3,2,1,0:T(4,128)(2,1)}), bf16[128,3,4,128]{3,2,1,0:T(4,128)(2,1)S(1)}, u32[]{:S(2)}, u32[]{:S(2)}) async-start(bf16[128,3,4,128]{3,2,1,0:T(4,128)(2,1)} %bitcast.8), calls=%async_computation | async-start | bytes 786432 | tf_op jit(solution)/shard_map/all_to_all | solution.py:358
  33.1 0.0 collective-permute-done
  33.1 0.0 collective-permute-done.1
  33.1 7.4 %collective-permute-start.3 = (bf16[4,144,128]{2,1,0:T(8,128)(2,1)S(1)}, bf16[4,144,128]{2,1,0:T(8,128)(2,1)S(1)}, u32[]{:S(2)}, u32[]{:S(2)}) collective-permute-start(bf16[4,144,128]{2,1,0:T(8,128)(2,1)S(1)} %pad_maximum_fusion.own_ref), channel_id=1, source_target_pairs={{1,2},{3,4},{5,6},{7,8},{9,10},{11,12},{13,14},{15,16},{17,18},{19... | collective-permute-start | bytes 442376 | tf_op jit(solution)/shard_map/ppermute | solution.py:343
  40.5 1.9 %collective-permute-start.2 = (bf16[4,144,128]{2,1,0:T(8,128)(2,1)S(1)}, bf16[4,144,128]{2,1,0:T(8,128)(2,1)S(1)}, u32[]{:S(2)}, u32[]{:S(2)}) collective-permute-start(bf16[4,144,128]{2,1,0:T(8,128)(2,1)S(1)} %pad_maximum_fusion.own_ref), channel_id=1, source_target_pairs={{0,1},{2,3},{4,5},{6,7},{8,9},{10,11},{12,13},{14,15},{16,17},{18,... | collective-permute-start | bytes 442376 | tf_op jit(solution)/shard_map/ppermute | solution.py:343
  42.4 1.9 %collective-permute-start.4 = (bf16[1,128,128]{2,1,0:T(8,128)(2,1)S(1)}, bf16[1,128,128]{2,1,0:T(8,128)(2,1)S(1)}, u32[]{:S(2)}, u32[]{:S(2)}) collective-permute-start(bf16[1,128,128]{2,1,0:T(8,128)(2,1)S(1)} %get-tuple-element.20), channel_id=1, source_target_pairs={{0,2},{1,3},{4,6},{5,7},{8,10},{9,11},{12,14},{13,15},{16,18},{17,... | collective-permute-start | bytes 98312 | tf_op jit(solution)/shard_map/ppermute | solution.py:343
  44.4 5.1 %collective-permute-start.5 = (bf16[1,128,128]{2,1,0:T(8,128)(2,1)S(1)}, bf16[1,128,128]{2,1,0:T(8,128)(2,1)S(1)}, u32[]{:S(2)}, u32[]{:S(2)}) collective-permute-start(bf16[1,128,128]{2,1,0:T(8,128)(2,1)S(1)} %get-tuple-element.21), channel_id=1, source_target_pairs={{2,4},{3,5},{6,8},{7,9},{10,12},{11,13},{14,16},{15,17},{18,20},{1... | collective-permute-start | bytes 98312 | tf_op jit(solution)/shard_map/ppermute | solution.py:343
  49.5 1.3 %collective-permute-done.4.far0_ref = bf16[1,128,128]{2,1,0:T(8,128)(2,1)S(1)} collective-permute-done((bf16[1,128,128]{2,1,0:T(8,128)(2,1)S(1)}, bf16[1,128,128]{2,1,0:T(8,128)(2,1)S(1)}, u32[]{:S(2)}, u32[]{:S(2)}) %collective-permute-start.4) | collective-permute-done | bytes 32800 | tf_op jit(solution)/shard_map/ppermute | solution.py:343
  50.8 4.2 %collective-permute-done.5.far1_ref = bf16[1,128,128]{2,1,0:T(8,128)(2,1)S(1)} collective-permute-done((bf16[1,128,128]{2,1,0:T(8,128)(2,1)S(1)}, bf16[1,128,128]{2,1,0:T(8,128)(2,1)S(1)}, u32[]{:S(2)}, u32[]{:S(2)}) %collective-permute-start.5) | collective-permute-done | bytes 32800 | tf_op jit(solution)/shard_map/ppermute | solution.py:343
  55.0 0.0 collective-permute-done.3.near1_ref
  55.0 0.0 collective-permute-done.2.near0_ref
  55.0 0.0 all-to-all-done
  55.0 15.2 %window.1 = (bf16[3,4,100,128]{3,2,1,0:T(8,128)(2,1)S(1)}, bf16[512,128]{1,0:T(8,128)(2,1)}) custom-call(s32[1]{0:T(128)} %bitcast.m_ref, s32[1]{0:T(128)} %bitcast.1.lon_ref, bf16[4,144,128]{2,1,0:T(8,128)(2,1)S(1)} %pad_maximum_fusion.own_ref, bf16[4,144,128]{2,1,0:T(8,128)(2,1)S(1)} %collective-permute-done.2.near0_ref, ...), custom_call_target="tpu_custom_call" | custom-call | tf_op jit(solution)/shard_map/window/pallas_call | solution.py:363
  70.2 10.9 %all-to-all-start.2 = ((bf16[128,4,128]{2,1,0:T(4,128)(2,1)}), bf16[128,4,128]{2,1,0:T(4,128)(2,1)S(1)}, u32[]{:S(2)}, u32[]{:S(2)}) async-start(bf16[128,4,128]{2,1,0:T(4,128)(2,1)} %bitcast.14), calls=%async_computation.2 | async-start | bytes 262144 | tf_op jit(solution)/shard_map/all_to_all | solution.py:390
  81.1 0.8 copy.17
  81.9 0.7 copy.18
  82.6 12.1 %all-to-all-done.2 = bf16[128,4,128]{2,1,0:T(4,128)(2,1)S(1)} async-done(((bf16[128,4,128]{2,1,0:T(4,128)(2,1)}), bf16[128,4,128]{2,1,0:T(4,128)(2,1)S(1)}, u32[]{:S(2)}, u32[]{:S(2)}) %all-to-all-start.2) | async-done | bytes 131104 | tf_op jit(solution)/shard_map/all_to_all | solution.py:390
  94.6 0.9 result.1
  (8 shorter events, 0.1 us)
Async XLA Ops:
  2.3 5.0 %copy-start.2 = (f32[100,4,128]{2,1,0:T(4,128)S(1)}, f32[100,4,128]{2,1,0:T(4,128)}, u32[]{:S(2)}) copy-start(f32[100,4,128]{2,1,0:T(4,128)} %temp_ref.1) | copy-start | bytes 614404
  2.3 16.1 %copy-start.3 = (f32[256,100]{0,1:T(8,128)S(1)}, f32[256,100]{0,1:T(8,128)}, u32[]{:S(2)}) copy-start(f32[256,100]{0,1:T(8,128)} %param.22) | copy-start | bytes 307204
  2.3 18.1 %all-to-all-start.1 = ((bf16[4,2,104,128]{3,2,1,0:T(8,128)(2,1)}), bf16[4,2,104,128]{3,2,1,0:T(8,128)(2,1)S(1)}, u32[]{:S(2)}, u32[]{:S(2)}) async-start(bf16[4,2,104,128]{3,2,1,0:T(8,128)(2,1)} %mixes.1), calls=%async_computation.1 | async-start | bytes 425984 | tf_op jit(solution)/shard_map/all_to_all | solution.py:311
  7.3 0.7 copy-start.4
  7.9 10.4 %copy-start = (f32[256,100]{0,1:T(8,128)S(1)}, f32[256,100]{0,1:T(8,128)}, u32[]{:S(2)}) copy-start(f32[256,100]{0,1:T(8,128)} %param.21) | copy-start | bytes 307204
  7.9 10.5 %copy-start.1 = (f32[256,100]{0,1:T(8,128)S(1)}, f32[256,100]{0,1:T(8,128)}, u32[]{:S(2)}) copy-start(f32[256,100]{0,1:T(8,128)} %param.23) | copy-start | bytes 307204
  8.1 24.9 %collective-permute-start = (bf16[4,8,128]{2,1,0:T(8,128)(2,1)S(1)}, bf16[4,8,128]{2,1,0:T(8,128)(2,1)S(1)}, u32[]{:S(2)}, u32[]{:S(2)}) collective-permute-start(bf16[4,8,128]{2,1,0:T(8,128)(2,1)S(1)} %get-tuple-element.18), channel_id=1, source_target_pairs={{32,64},{64,32},{33,65},{65,33},{34,66},{66,34},{35,67},{67,35},{3... | collective-permute-start | bytes 24584 | tf_op jit(solution)/shard_map/ppermute | solution.py:333
  16.4 16.6 %collective-permute-start.1 = (bf16[4,8,128]{2,1,0:T(8,128)(2,1)S(1)}, bf16[4,8,128]{2,1,0:T(8,128)(2,1)S(1)}, u32[]{:S(2)}, u32[]{:S(2)}) collective-permute-start(bf16[4,8,128]{2,1,0:T(8,128)(2,1)S(1)} %get-tuple-element.19), channel_id=1, source_target_pairs={{0,32},{32,0},{64,96},{96,64},{1,33},{33,1},{65,97},{97,65},{2,34}... | collective-permute-start | bytes 24584 | tf_op jit(solution)/shard_map/ppermute | solution.py:334
  20.4 34.7 %all-to-all-start = ((bf16[128,3,4,128]{3,2,1,0:T(4,128)(2,1)}), bf16[128,3,4,128]{3,2,1,0:T(4,128)(2,1)S(1)}, u32[]{:S(2)}, u32[]{:S(2)}) async-start(bf16[128,3,4,128]{3,2,1,0:T(4,128)(2,1)} %bitcast.8), calls=%async_computation | async-start | bytes 786432 | tf_op jit(solution)/shard_map/all_to_all | solution.py:358
  33.1 21.9 %collective-permute-start.3 = (bf16[4,144,128]{2,1,0:T(8,128)(2,1)S(1)}, bf16[4,144,128]{2,1,0:T(8,128)(2,1)S(1)}, u32[]{:S(2)}, u32[]{:S(2)}) collective-permute-start(bf16[4,144,128]{2,1,0:T(8,128)(2,1)S(1)} %pad_maximum_fusion.own_ref), channel_id=1, source_target_pairs={{1,2},{3,4},{5,6},{7,8},{9,10},{11,12},{13,14},{15,16},{17,18},{19... | collective-permute-start | bytes 442376 | tf_op jit(solution)/shard_map/ppermute | solution.py:343
  40.5 14.5 %collective-permute-start.2 = (bf16[4,144,128]{2,1,0:T(8,128)(2,1)S(1)}, bf16[4,144,128]{2,1,0:T(8,128)(2,1)S(1)}, u32[]{:S(2)}, u32[]{:S(2)}) collective-permute-start(bf16[4,144,128]{2,1,0:T(8,128)(2,1)S(1)} %pad_maximum_fusion.own_ref), channel_id=1, source_target_pairs={{0,1},{2,3},{4,5},{6,7},{8,9},{10,11},{12,13},{14,15},{16,17},{18,... | collective-permute-start | bytes 442376 | tf_op jit(solution)/shard_map/ppermute | solution.py:343
  42.4 8.4 %collective-permute-start.4 = (bf16[1,128,128]{2,1,0:T(8,128)(2,1)S(1)}, bf16[1,128,128]{2,1,0:T(8,128)(2,1)S(1)}, u32[]{:S(2)}, u32[]{:S(2)}) collective-permute-start(bf16[1,128,128]{2,1,0:T(8,128)(2,1)S(1)} %get-tuple-element.20), channel_id=1, source_target_pairs={{0,2},{1,3},{4,6},{5,7},{8,10},{9,11},{12,14},{13,15},{16,18},{17,... | collective-permute-start | bytes 98312 | tf_op jit(solution)/shard_map/ppermute | solution.py:343
  44.4 10.7 %collective-permute-start.5 = (bf16[1,128,128]{2,1,0:T(8,128)(2,1)S(1)}, bf16[1,128,128]{2,1,0:T(8,128)(2,1)S(1)}, u32[]{:S(2)}, u32[]{:S(2)}) collective-permute-start(bf16[1,128,128]{2,1,0:T(8,128)(2,1)S(1)} %get-tuple-element.21), channel_id=1, source_target_pairs={{2,4},{3,5},{6,8},{7,9},{10,12},{11,13},{14,16},{15,17},{18,20},{1... | collective-permute-start | bytes 98312 | tf_op jit(solution)/shard_map/ppermute | solution.py:343
  70.2 24.4 %all-to-all-start.2 = ((bf16[128,4,128]{2,1,0:T(4,128)(2,1)}), bf16[128,4,128]{2,1,0:T(4,128)(2,1)S(1)}, u32[]{:S(2)}, u32[]{:S(2)}) async-start(bf16[128,4,128]{2,1,0:T(4,128)(2,1)} %bitcast.14), calls=%async_computation.2 | async-start | bytes 262144 | tf_op jit(solution)/shard_map/all_to_all | solution.py:390
